TPU v7x, 32 devices: a whole 2x2x4 slice. The times are simulated.
32 devices in a mesh: ctx: 8 (over z, y), wsh: 4 (over x, core).
Axes of the slice: x: 2, y: 2, z: 4, core: 2. Of those that a mesh axis runs over, the one named last changes fastest.
Arguments:
- tokens: bfloat16 [8, 1024, 1024], P('wsh', 'ctx'), may hold values from -6 to 6
- routes: int32 [8, 1024, 8], P('wsh', 'ctx'), may hold values from 0 to 31, all different within a row; in each aligned block of 128 rows (0 to 127, 128 to 255, ..., all dimensions but the last counted through in order) at most 48 rows name the same one
- in_weight: bfloat16 [1024, 2048], replicated, may hold values from -0.1875 to 0.1875
- out_weight: bfloat16 [1024, 1024], replicated, may hold values from -0.75 to 0.75
- first_gain: float32 [1024], replicated, may hold values from 0.5 to 1.5
- second_gain: float32 [1024], replicated, may hold values from 0.5 to 1.5
- router_weight: bfloat16 [1024, 32], replicated, may hold values from -0.1875 to 0.1875
- gate_weight: bfloat16 [32, 1024, 512], P('ctx', None, 'wsh'), may hold values from -0.1875 to 0.1875
- up_weight: bfloat16 [32, 1024, 512], P('ctx', None, 'wsh'), may hold values from -0.1875 to 0.1875
- down_weight: bfloat16 [32, 512, 1024], P('ctx', 'wsh'), may hold values from -0.75 to 0.75
- cotangent: bfloat16 [8, 1024, 1024], P('wsh', 'ctx'), may hold values from -6 to 6
Outputs:
- layer_out: bfloat16 [8, 1024, 1024], P('wsh', 'ctx')
- tokens_grad: bfloat16 [8, 1024, 1024], P('wsh', 'ctx')
- in_grad: float32 [1024, 2048], P(('ctx', 'wsh'))
- out_grad: float32 [1024, 1024], P(('ctx', 'wsh'))
- first_gain_grad: float32 [1024], P(('ctx', 'wsh'))
- second_gain_grad: float32 [1024], P(('ctx', 'wsh'))
- router_grad: float32 [1024, 32], P(('ctx', 'wsh'))
- gate_grad: float32 [32, 1024, 512], P('ctx', None, 'wsh')
- up_grad: float32 [32, 1024, 512], P('ctx', None, 'wsh')
- down_grad: float32 [32, 512, 1024], P('ctx', 'wsh')
Inputs may be any that keep to these rules, and one draw needn't show every extreme that they name: `routes`: in each aligned block of 128 rows (one sequence's rows on one index of ctx) the 8 experts of a row differ, and no expert is named by more than 48 rows of the block; some block reaches 48.
All inputs are finite; a program needn't handle non-finite values.
Results may differ from a plain program's by a relative error of at most 0.018.
Values may be sent and summed in bfloat16 or wider, within the bound.
No kernel may reach another device: no remote copies, remote signals or barrier semaphores. Data moves between devices by JAX's collectives and lax.ppermute only.
A program may use at most 256 MiB of HBM per device.

v0:
```python
import math

import jax
import jax.numpy as jnp
from jax import lax
from jax.sharding import PartitionSpec as P

D = 1024
HEADS = 16
KV_HEADS = 8
HEAD_DIM = 64
EXPERTS = 32
TOP = 8
SEQ_TOK = 128
SEQ_GRP = 2
HALF = 64
MOST = 48


EPS = 1e-05
THETA = 10000.0
NEG = -1e30


def dealt(rows, length):
    owner = rows // SEQ_TOK
    offset = rows % SEQ_TOK
    early = owner * HALF + offset
    late = length - (owner + 1) * HALF + offset - HALF
    return jnp.where(offset < HALF, early, late)


def rotate(values, place, sign):
    half_dim = values.shape[-1] // 2
    freq = THETA ** (-2.0 * jnp.arange(half_dim, dtype=jnp.float32) / values.shape[-1])
    angle = place.astype(jnp.float32)[:, None] * freq[None, :]
    cosine = jnp.cos(angle)[:, None, :]
    sine = sign * jnp.sin(angle)[:, None, :]
    front = values[..., :half_dim]
    back = values[..., half_dim:]
    return jnp.concatenate([front * cosine - back * sine, back * cosine + front * sine], -1)


def norm_back(values, scale, gain, grad_out):
    weighted = grad_out * gain
    grad_in = scale * weighted - values * scale**3 * jnp.mean(weighted * values, -1, keepdims=True)
    return (grad_in, jnp.sum(grad_out * values * scale, 0))


def split_block(block):
    width_k = KV_HEADS * HEAD_DIM
    size = block.shape[0]
    keys = block[..., :width_k].reshape(size, SEQ_GRP, KV_HEADS, HEAD_DIM)
    values = block[..., width_k:].reshape(size, SEQ_GRP, KV_HEADS, HEAD_DIM)
    return (keys, values)


def block_scores(query, keys, query_place, key_place):
    scores = jnp.einsum(
        "sqngd,ksnd->sngqk", query, keys, preferred_element_type=jnp.float32
    ) * HEAD_DIM ** (-0.5)
    allowed = key_place[None, :] <= query_place[:, None]
    return (scores, allowed)


def stack_blocks(whole, places):
    size = math.gcd(whole.shape[0], 512)
    count = whole.shape[0] // size
    return (whole.reshape(count, size, SEQ_GRP, whole.shape[-1]), places.reshape(count, size))


def attend(query, whole, query_place, places):
    group = HEADS // KV_HEADS
    stacked, block_places = stack_blocks(whole, places)
    shape = (SEQ_GRP, KV_HEADS, group, SEQ_TOK)

    def max_step(carry, item):
        peak, total = carry
        keys, values = split_block(item[0])
        scores, allowed = block_scores(query, keys, query_place, item[1])
        masked = jnp.where(allowed, scores, NEG)
        new_peak = jnp.maximum(peak, jnp.max(masked, -1))
        weights = jnp.where(allowed, jnp.exp(masked - new_peak[..., None]), 0.0)
        total = total * jnp.exp(peak - new_peak) + jnp.sum(weights, -1)
        return ((new_peak, total), None)

    start = (jnp.full(shape, NEG, jnp.float32), jnp.zeros(shape, jnp.float32))
    (peak, total), unused = lax.scan(max_step, start, (stacked, block_places))
    log_total = peak + jnp.log(total)

    def value_step(accum, item):
        keys, values = split_block(item[0])
        scores, allowed = block_scores(query, keys, query_place, item[1])
        probs = jnp.where(allowed, jnp.exp(scores - log_total[..., None]), 0.0).astype(jnp.bfloat16)
        return (
            accum
            + jnp.einsum("sngqk,ksnd->sqngd", probs, values, preferred_element_type=jnp.float32),
            None,
        )

    empty = jnp.zeros((SEQ_GRP, SEQ_TOK, KV_HEADS, group, HEAD_DIM), jnp.float32)
    attended, unused = lax.scan(value_step, empty, (stacked, block_places))
    return (attended, log_total)


def score_grads(query, grad_out, log_total, delta, keys, values, query_place, key_place):
    scores, allowed = block_scores(query, keys, query_place, key_place)
    probs = jnp.where(allowed, jnp.exp(scores - log_total[..., None]), 0.0)
    grad_probs = jnp.einsum(
        "sqngd,ksnd->sngqk", grad_out, values, preferred_element_type=jnp.float32
    )
    grad_scores = (probs * (grad_probs - delta[..., None])).astype(jnp.bfloat16)
    return (probs, grad_scores)


def query_grads(query, grad_out, log_total, delta, whole, query_place, places):
    stacked, block_places = stack_blocks(whole, places)

    def query_step(accum, item):
        keys, values = split_block(item[0])
        probs, grad_scores = score_grads(
            query, grad_out, log_total, delta, keys, values, query_place, item[1]
        )
        return (
            accum
            + jnp.einsum(
                "sngqk,ksnd->sqngd", grad_scores, keys, preferred_element_type=jnp.float32
            ),
            None,
        )

    accum, unused = lax.scan(
        query_step, jnp.zeros(query.shape, jnp.float32), (stacked, block_places)
    )
    return accum * HEAD_DIM ** (-0.5)


def key_value_block(query, grad_out, log_total, delta, query_place, block, key_place):
    keys, values = split_block(block)
    probs, grad_scores = score_grads(
        query, grad_out, log_total, delta, keys, values, query_place, key_place
    )
    grad_keys = jnp.einsum(
        "sngqk,sqngd->ksnd", grad_scores, query, preferred_element_type=jnp.float32
    ) * HEAD_DIM ** (-0.5)
    grad_values = jnp.einsum(
        "sngqk,sqngd->ksnd",
        probs.astype(jnp.bfloat16),
        grad_out,
        preferred_element_type=jnp.float32,
    )
    size = block.shape[0]
    return jnp.concatenate(
        [grad_keys.reshape(size, SEQ_GRP, -1), grad_values.reshape(size, SEQ_GRP, -1)], -1
    )


def shards(
    tokens,
    routes,
    in_weight,
    out_weight,
    first_gain,
    second_gain,
    router_weight,
    gate_weight,
    up_weight,
    down_weight,
    cotangent,
):
    ctx_count = lax.axis_size("ctx")
    length = SEQ_TOK * ctx_count
    rows = SEQ_GRP * SEQ_TOK
    group = HEADS // KV_HEADS
    width_q = HEADS * HEAD_DIM
    width_k = KV_HEADS * HEAD_DIM
    my_index = lax.axis_index("ctx")
    local_place = dealt(my_index * SEQ_TOK + jnp.arange(SEQ_TOK, dtype=jnp.int32), length)
    all_place = dealt(jnp.arange(length, dtype=jnp.int32), length)
    inputs = tokens.astype(jnp.float32).reshape(rows, D)
    scale_one = lax.rsqrt(jnp.mean(inputs * inputs, -1, keepdims=True) + EPS)
    normed = (inputs * scale_one * first_gain).astype(jnp.bfloat16)
    mixed = jnp.dot(normed, in_weight, preferred_element_type=jnp.float32).reshape(
        SEQ_GRP, SEQ_TOK, -1
    )
    query = rotate(
        mixed[..., :width_q].reshape(SEQ_GRP, SEQ_TOK, HEADS, HEAD_DIM), local_place, 1.0
    ).astype(jnp.bfloat16)
    query = query.reshape(SEQ_GRP, SEQ_TOK, KV_HEADS, group, HEAD_DIM)
    key = rotate(
        mixed[..., width_q : width_q + width_k].reshape(SEQ_GRP, SEQ_TOK, KV_HEADS, HEAD_DIM),
        local_place,
        1.0,
    ).astype(jnp.bfloat16)
    value = mixed[..., width_q + width_k :].astype(jnp.bfloat16)
    key_value = jnp.swapaxes(
        jnp.concatenate([key.reshape(SEQ_GRP, SEQ_TOK, width_k), value], -1), 0, 1
    )
    whole = lax.all_gather(key_value, "ctx", axis=0, tiled=True)
    attended_full, log_total = attend(query, whole, local_place, all_place)
    attended = attended_full.reshape(rows, width_q).astype(jnp.bfloat16)
    resid = inputs + jnp.dot(attended, out_weight, preferred_element_type=jnp.float32)
    scale_two = lax.rsqrt(jnp.mean(resid * resid, -1, keepdims=True) + EPS)
    normed_two = (resid * scale_two * second_gain).astype(jnp.bfloat16)
    logits = jnp.dot(normed_two, router_weight, preferred_element_type=jnp.float32)
    route_rows = routes.reshape(rows, TOP)
    chosen = route_rows[..., None] == jnp.arange(EXPERTS, dtype=jnp.int32)
    picked = jnp.sum(jnp.where(chosen, logits[:, None, :], 0.0), -1)
    gates = jax.nn.softmax(picked, -1)
    gates_low = gates.astype(jnp.bfloat16)
    counts = chosen.reshape(SEQ_GRP, SEQ_TOK * TOP, EXPERTS).astype(jnp.int32)
    ranks = jnp.sum((jnp.cumsum(counts, 1) - 1) * counts, -1).reshape(rows, TOP)
    owner = (jnp.arange(rows, dtype=jnp.int32) // SEQ_TOK)[:, None]
    slots = (owner * MOST + ranks) * EXPERTS + route_rows
    slot_count = SEQ_GRP * MOST * EXPERTS
    slot_ids = jnp.arange(slot_count, dtype=jnp.int32)[:, None]
    dispatch = jnp.zeros((slot_count, rows), jnp.bfloat16)
    combine = jnp.zeros((slot_count, rows), jnp.bfloat16)
    for route_index in range(TOP):
        match = slot_ids == slots[None, :, route_index]
        dispatch = dispatch + match.astype(jnp.bfloat16)
        combine = combine + jnp.where(
            match, gates_low[None, :, route_index], jnp.zeros((), jnp.bfloat16)
        )
    sending = jnp.dot(dispatch, normed_two, preferred_element_type=jnp.float32).astype(jnp.bfloat16)
    sending = sending.reshape(SEQ_GRP, MOST, EXPERTS, D)
    arrived = lax.all_to_all(sending, "ctx", split_axis=2, concat_axis=0, tiled=True)
    gate_full, up_full, down_full = (
        lax.all_gather(gate_weight, "wsh", axis=2, tiled=True),
        lax.all_gather(up_weight, "wsh", axis=2, tiled=True),
        lax.all_gather(down_weight, "wsh", axis=1, tiled=True),
    )
    gate_act = jnp.einsum("rmxd,xdf->rmxf", arrived, gate_full, preferred_element_type=jnp.float32)
    up_act = jnp.einsum("rmxd,xdf->rmxf", arrived, up_full, preferred_element_type=jnp.float32)
    sigma = jax.nn.sigmoid(gate_act)
    swish = gate_act * sigma
    hidden = (swish * up_act).astype(jnp.bfloat16)
    produced = jnp.einsum(
        "rmxf,xfd->rmxd", hidden, down_full, preferred_element_type=jnp.float32
    ).astype(jnp.bfloat16)
    returned = lax.all_to_all(produced, "ctx", split_axis=0, concat_axis=2, tiled=True)
    returned_flat = returned.reshape(slot_count, D)
    mixture = lax.dot_general(
        combine, returned_flat, (((0,), (0,)), ((), ())), preferred_element_type=jnp.float32
    )
    layer_out = (resid + mixture).astype(jnp.bfloat16).reshape(SEQ_GRP, SEQ_TOK, D)
    upstream = cotangent.reshape(rows, D)
    grad_returned = jnp.dot(combine, upstream, preferred_element_type=jnp.float32).astype(
        jnp.bfloat16
    )
    grad_produced = lax.all_to_all(
        grad_returned.reshape(SEQ_GRP, MOST, EXPERTS, D),
        "ctx",
        split_axis=2,
        concat_axis=0,
        tiled=True,
    )
    down_local = jnp.einsum(
        "rmxf,rmxd->xfd", hidden, grad_produced, preferred_element_type=jnp.float32
    )
    grad_hidden = jnp.einsum(
        "rmxd,xfd->rmxf", grad_produced, down_full, preferred_element_type=jnp.float32
    ).astype(jnp.bfloat16)
    slope = sigma * (1.0 + gate_act * (1.0 - sigma))
    grad_gate = (grad_hidden * up_act * slope).astype(jnp.bfloat16)
    grad_up = (grad_hidden * swish).astype(jnp.bfloat16)
    gate_local = jnp.einsum(
        "rmxd,rmxf->xdf", arrived, grad_gate, preferred_element_type=jnp.float32
    )
    up_local = jnp.einsum("rmxd,rmxf->xdf", arrived, grad_up, preferred_element_type=jnp.float32)
    grad_arrived = jnp.einsum(
        "rmxf,xdf->rmxd", grad_gate, gate_full, preferred_element_type=jnp.float32
    )
    grad_arrived = (
        grad_arrived
        + jnp.einsum("rmxf,xdf->rmxd", grad_up, up_full, preferred_element_type=jnp.float32)
    ).astype(jnp.bfloat16)
    grad_sent = lax.all_to_all(grad_arrived, "ctx", split_axis=0, concat_axis=2, tiled=True)
    gate_grad, up_grad, down_grad = (
        lax.psum_scatter(
            gate_local.astype(jnp.bfloat16), "wsh", scatter_dimension=2, tiled=True
        ).astype(jnp.float32),
        lax.psum_scatter(
            up_local.astype(jnp.bfloat16), "wsh", scatter_dimension=2, tiled=True
        ).astype(jnp.float32),
        lax.psum_scatter(
            down_local.astype(jnp.bfloat16), "wsh", scatter_dimension=1, tiled=True
        ).astype(jnp.float32),
    )
    grad_normed_two = lax.dot_general(
        dispatch,
        grad_sent.reshape(slot_count, D),
        (((0,), (0,)), ((), ())),
        preferred_element_type=jnp.float32,
    )
    picked_rows = jnp.take(returned_flat, slots.reshape(-1), axis=0).reshape(rows, TOP, D)
    grad_gates = jnp.einsum("tkd,td->tk", picked_rows, upstream, preferred_element_type=jnp.float32)
    grad_picked = gates * (grad_gates - jnp.sum(gates * grad_gates, -1, keepdims=True))
    grad_logits = jnp.sum(jnp.where(chosen, grad_picked[..., None], 0.0), 1).astype(jnp.bfloat16)
    router_local = lax.dot_general(
        normed_two, grad_logits, (((0,), (0,)), ((), ())), preferred_element_type=jnp.float32
    )
    grad_normed_two = grad_normed_two + lax.dot_general(
        grad_logits, router_weight, (((1,), (1,)), ((), ())), preferred_element_type=jnp.float32
    )
    grad_resid_norm, second_local = norm_back(resid, scale_two, second_gain, grad_normed_two)
    grad_resid = upstream.astype(jnp.float32) + grad_resid_norm
    grad_branch = grad_resid.astype(jnp.bfloat16)
    out_local = lax.dot_general(
        attended, grad_branch, (((0,), (0,)), ((), ())), preferred_element_type=jnp.float32
    )
    grad_attended = lax.dot_general(
        grad_branch, out_weight, (((1,), (1,)), ((), ())), preferred_element_type=jnp.float32
    ).astype(jnp.bfloat16)
    grad_out = grad_attended.reshape(SEQ_GRP, SEQ_TOK, KV_HEADS, group, HEAD_DIM)
    delta = jnp.einsum("sqngd,sqngd->sngq", grad_out.astype(jnp.float32), attended_full)
    grad_query = query_grads(query, grad_out, log_total, delta, whole, local_place, all_place)
    size = math.gcd(SEQ_TOK * lax.axis_size("ctx"), 512)
    pieces = SEQ_TOK * lax.axis_size("ctx") // size

    def block_term(item):
        return key_value_block(query, grad_out, log_total, delta, local_place, item[0], item[1])

    terms = lax.map(
        block_term,
        (whole.reshape(pieces, size, SEQ_GRP, whole.shape[-1]), all_place.reshape(pieces, size)),
    )
    kv_grad = jnp.swapaxes(
        lax.psum_scatter(
            terms.reshape(SEQ_TOK * lax.axis_size("ctx"), SEQ_GRP, terms.shape[-1]).astype(
                jnp.bfloat16
            ),
            "ctx",
            scatter_dimension=0,
            tiled=True,
        ).astype(jnp.float32),
        0,
        1,
    )
    grad_query = rotate(grad_query.reshape(SEQ_GRP, SEQ_TOK, HEADS, HEAD_DIM), local_place, -1.0)
    grad_key = rotate(
        kv_grad[..., :width_k].reshape(SEQ_GRP, SEQ_TOK, KV_HEADS, HEAD_DIM), local_place, -1.0
    )
    grad_mixed = jnp.concatenate(
        [
            grad_query.reshape(SEQ_GRP, SEQ_TOK, width_q),
            grad_key.reshape(SEQ_GRP, SEQ_TOK, width_k),
            kv_grad[..., width_k:],
        ],
        -1,
    )
    grad_mixed = grad_mixed.astype(jnp.bfloat16).reshape(rows, -1)
    in_local = lax.dot_general(
        normed, grad_mixed, (((0,), (0,)), ((), ())), preferred_element_type=jnp.float32
    )
    grad_normed = lax.dot_general(
        grad_mixed, in_weight, (((1,), (1,)), ((), ())), preferred_element_type=jnp.float32
    )
    grad_inputs_norm, first_local = norm_back(inputs, scale_one, first_gain, grad_normed)
    tokens_grad = (grad_resid + grad_inputs_norm).astype(jnp.bfloat16).reshape(SEQ_GRP, SEQ_TOK, D)
    in_grad, out_grad, first_gain_grad, second_gain_grad, router_grad = (
        lax.psum_scatter(in_local, ("ctx", "wsh"), scatter_dimension=0, tiled=True),
        lax.psum_scatter(out_local, ("ctx", "wsh"), scatter_dimension=0, tiled=True),
        lax.psum_scatter(first_local, ("ctx", "wsh"), scatter_dimension=0, tiled=True),
        lax.psum_scatter(second_local, ("ctx", "wsh"), scatter_dimension=0, tiled=True),
        lax.psum_scatter(router_local, ("ctx", "wsh"), scatter_dimension=0, tiled=True),
    )
    return (
        layer_out,
        tokens_grad,
        in_grad,
        out_grad,
        first_gain_grad,
        second_gain_grad,
        router_grad,
        gate_grad,
        up_grad,
        down_grad,
    )


def solution(mesh):
    placed = (
        P("wsh", "ctx", None),
        P("wsh", "ctx", None),
        P(),
        P(),
        P(),
        P(),
        P(),
        P("ctx", None, "wsh"),
        P("ctx", None, "wsh"),
        P("ctx", "wsh", None),
        P("wsh", "ctx", None),
    )
    return jax.shard_map(
        shards,
        mesh=mesh,
        in_specs=placed,
        out_specs=(
            P("wsh", "ctx", None),
            P("wsh", "ctx", None),
            P(("ctx", "wsh"), None),
            P(("ctx", "wsh"), None),
            P(("ctx", "wsh")),
            P(("ctx", "wsh")),
            P(("ctx", "wsh"), None),
            P("ctx", None, "wsh"),
            P("ctx", None, "wsh"),
            P("ctx", "wsh", None),
        ),
        check_vma=False,
    )
```

profile of v0, /device:TPU:0, one launch (start us, length us, event | category | flops | bytes accessed | tf_op | source)
XLA Modules:
  0.0 1509.2 jit_solution(4395678561090261945)
XLA Ops:
  18.8 31.3 %reduce-window.6 = s32[2,32,8,128]{3,2,1,0:T(8,128)S(1)} reduce-window(s32[2,32,8,128]{3,2,1,0:T(8,128)} %fusion.160, s32[]{:T(128)} %constant.168.clone.1), window={size=1x1x1x128 pad=0_0x0_0x0_0x127_0}, to_apply=%region_7.8 | reduce-window | flops 8323072 | bytes 524292 | tf_op jit(solution)/shard_map/reduce-window
  57.8 35.2 %all-gather.5.cloned.1.call-done = bf16[1024,2,1024]{2,0,1:T(8,128)(2,1)} async-done(((bf16[128,2,1024]{2,0,1:T(8,128)(2,1)}), bf16[1024,2,1024]{2,0,1:T(8,128)(2,1)}) %all-gather.5.cloned.1.call-update) | async-done | bytes 4194320 | tf_op jit(solution)/shard_map/all_gather | solution.py:199
  99.2 11.3 while.47
  110.5 16.9 %while.48 = (s32[]{:T(128)}, f32[2,128,8,2,64]{1,4,3,2,0:T(8,128)}, bf16[2,512,2,1024]{1,3,2,0:T(8,128)(2,1)}, s32[2,512]{1,0:T(2,128)S(1)}, bf16[2,128,8,2,64]{...) while((s32[]{:T(128)}, f32[2,128,8,2,64]{1,4,3,2,0:T(8,128)}, ...), condition=%wide.region_6.7_spmd.clone, body=%wide.region_5.6_spmd.clone.sunk | while | flops 545853056 | bytes 13261947 | solution.py:102
  159.0 126.6 %all-to-all-done.2 = bf16[2,48,32,1024]{3,1,0,2:T(8,128)(2,1)} async-done(((bf16[2,48,32,1024]{3,1,0,2:T(8,128)(2,1)}), bf16[2,48,32,1024]{3,1,0,2:T(8,128)(2,1)}, u32[]{:S(2)}, u32[]{:S(2)}) %all-to-all-start.2) | async-done | bytes 6291488 | tf_op jit(solution)/shard_map/all_to_all | solution.py:251
  298.2 129.4 %all-to-all-done = bf16[2,48,32,1024]{3,1,0,2:T(8,128)(2,1)} async-done(((bf16[2,48,32,1024]{3,1,0,2:T(8,128)(2,1)}), bf16[2,48,32,1024]{3,1,0,2:T(8,128)(2,1)}, u32[]{:S(2)}, u32[]{:S(2)}) %all-to-all-start) | async-done | bytes 6291488 | tf_op jit(solution)/shard_map/all_to_all | solution.py:227
  434.4 10.0 fusion.83
  444.4 10.1 fusion.79
  454.5 13.3 fusion.68
  481.6 12.9 fusion.77
  494.5 12.8 fusion.66
  514.0 104.8 %all-to-all-done.1 = bf16[16,48,4,1024]{3,1,2,0:T(8,128)(2,1)} async-done(((bf16[16,48,4,1024]{3,1,2,0:T(8,128)(2,1)}), bf16[16,48,4,1024]{3,1,2,0:T(8,128)(2,1)}, u32[]{:S(2)}, u32[]{:S(2)}) %all-to-all-start.1) | async-done | bytes 6291488 | tf_op jit(solution)/shard_map/all_to_all | solution.py:241
  624.2 10.2 copy.246
  634.5 9.9 reshape.459
  644.4 14.6 gather_fusion
  664.5 96.4 %all-to-all-done.3 = bf16[16,48,4,1024]{3,1,2,0:T(8,128)(2,1)} async-done(((bf16[16,48,4,1024]{3,1,2,0:T(8,128)(2,1)}), bf16[16,48,4,1024]{3,1,2,0:T(8,128)(2,1)}, u32[]{:S(2)}, u32[]{:S(2)}) %all-to-all-start.3) | async-done | bytes 6291488 | tf_op jit(solution)/shard_map/all_to_all | solution.py:278
  760.9 10.3 copy.245
  771.2 10.1 reshape.463
  792.9 51.0 %while.46 = (s32[]{:T(128)}, bf16[2,512,2,1024]{3,1,0,2:T(8,128)(2,1)}, s32[2,512]{1,0:T(2,128)S(1)}, bf16[2,512,2,1024]{1,3,2,0:T(8,128)(2,1)}, bf16[2,128,8,2,...) while((s32[]{:T(128)}, ...), condition=%wide.region_20.21_spmd.clone, body=%wide.region_19.20_spmd.clone.sunk | while | flops 1100025472 | bytes 56876184 | solution.py:324
  844.1 9.2 bitcast_convert_fusion.2
  853.2 8.2 copy.206
  868.1 11.5 bitcast_convert_fusion.1
  879.6 8.1 copy.208
  894.3 9.4 bitcast_convert_fusion
  909.2 33.2 %while.49 = (s32[]{:T(128)}, f32[2,128,8,2,64]{1,4,3,2,0:T(8,128)}, bf16[2,512,2,1024]{1,3,2,0:T(8,128)(2,1)}, s32[2,512]{1,0:T(2,128)S(1)}, bf16[2,128,8,2,64]{...) while((s32[]{:T(128)}, f32[2,128,8,2,64]{1,4,3,2,0:T(8,128)}, ...), condition=%wide.region_18.19_spmd.clone, body=%wide.region_17.18_spmd.clone.sunk | while | flops 818482816 | bytes 48405752 | solution.py:132
  956.7 21.6 %reduce-scatter.22.cloned.1.call-done = bf16[128,4096]{1,0:T(8,128)(2,1)} async-done(((bf16[512,4096]{1,0:T(8,128)(2,1)}), bf16[128,4096]{1,0:T(8,128)(2,1)}) %reduce-scatter.22.cloned.1.call-update) | async-done | bytes 1048592
  981.1 44.1 %reduce-scatter.24.cloned.1.call-done = bf16[128,4096]{1,0:T(8,128)(2,1)} async-done(((bf16[512,4096]{1,0:T(8,128)(2,1)}), bf16[128,4096]{1,0:T(8,128)(2,1)}) %reduce-scatter.24.cloned.1.call-update) | async-done | bytes 1048592
  1031.4 40.8 %reduce-scatter.20.cloned.1.call-done = bf16[4,128,1024]{2,1,0:T(8,128)(2,1)} async-done(((bf16[4,512,1024]{2,1,0:T(8,128)(2,1)}), bf16[4,128,1024]{2,1,0:T(8,128)(2,1)}) %reduce-scatter.20.cloned.1.call-update) | async-done | bytes 1048592 | tf_op jit(solution)/shard_map/reduce_scatter | solution.py:286
  1082.9 39.4 %all-reduce.2 = (f32[1024]{0:T(1024)S(1)}, f32[1024]{0:T(1024)S(1)}) all-reduce(f32[1024]{0:T(1024)S(1)} %get-tuple-element.454, f32[1024]{0:T(1024)S(1)} %copy-done.33), channel_id=5, replica_groups=mesh['ctx'=8,'wsh'=4] {'ctx','wsh'}, use_global_device_ids=true, to_apply=%region_26.27.clone | all-reduce | flops 2048 | bytes 16384
  1126.2 84.5 %reduce-scatter.18.cloned.1.call-done = f32[32,32]{1,0:T(8,128)} async-done(((f32[1024,32]{1,0:T(8,128)}), f32[32,32]{1,0:T(8,128)}) %reduce-scatter.18.cloned.1.call-update) | async-done | bytes 4112 | tf_op jit(solution)/shard_map/reduce_scatter | solution.py:366
  1210.8 141.8 %reduce-scatter.16.cloned.1.call-done = f32[32,1024]{1,0:T(8,128)} async-done(((f32[1024,1024]{1,0:T(8,128)}), f32[32,1024]{1,0:T(8,128)}) %reduce-scatter.16.cloned.1.call-update) | async-done | bytes 131088 | tf_op jit(solution)/shard_map/reduce_scatter | solution.py:363
  1352.6 148.8 %reduce-scatter.14.cloned.1.call-done = f32[32,2048]{1,0:T(8,128)} async-done(((f32[1024,2048]{1,0:T(8,128)}), f32[32,2048]{1,0:T(8,128)}) %reduce-scatter.14.cloned.1.call-update) | async-done | bytes 262160 | tf_op jit(solution)/shard_map/reduce_scatter | solution.py:362
  (372 shorter events, 286.1 us)
Async XLA Ops:
  8.0 121.3 %copy-start = (bf16[1024,1024]{1,0:T(8,128)(2,1)S(1)}, bf16[1024,1024]{1,0:T(8,128)(2,1)}, u32[]{:S(2)}) copy-start(bf16[1024,1024]{1,0:T(8,128)(2,1)} %param.22) | copy-start | bytes 6291460
  8.0 84.9 %all-gather.5.cloned.1.call-start = ((), (), s32[]{:S(2)}) async-start(), calls=%async_computation.11 | async-start | bytes 4718592 | tf_op jit(solution)/shard_map/all_gather | solution.py:199
  57.7 723.6 %copy-start.41 = (s32[256,1]{0,1:T(1,128)}, s32[256,1]{0,1:T(1,128)S(1)}, u32[]{:S(2)}) copy-start(s32[256,1]{0,1:T(1,128)S(1)} %get-tuple-element.553) | copy-start | bytes 3076
  57.7 723.6 %copy-start.43 = (s32[256,1]{0,1:T(1,128)}, s32[256,1]{0,1:T(1,128)S(1)}, u32[]{:S(2)}) copy-start(s32[256,1]{0,1:T(1,128)S(1)} %get-tuple-element.554) | copy-start | bytes 3076
  57.7 723.6 %copy-start.45 = (s32[256,1]{0,1:T(1,128)}, s32[256,1]{0,1:T(1,128)S(1)}, u32[]{:S(2)}) copy-start(s32[256,1]{0,1:T(1,128)S(1)} %get-tuple-element.555) | copy-start | bytes 3076
  57.7 723.6 %copy-start.47 = (s32[256,1]{0,1:T(1,128)}, s32[256,1]{0,1:T(1,128)S(1)}, u32[]{:S(2)}) copy-start(s32[256,1]{0,1:T(1,128)S(1)} %get-tuple-element.556) | copy-start | bytes 3076
  57.7 723.6 %copy-start.49 = (s32[256,1]{0,1:T(1,128)}, s32[256,1]{0,1:T(1,128)S(1)}, u32[]{:S(2)}) copy-start(s32[256,1]{0,1:T(1,128)S(1)} %get-tuple-element.557) | copy-start | bytes 3076
  57.7 723.6 %copy-start.51 = (s32[256,1]{0,1:T(1,128)}, s32[256,1]{0,1:T(1,128)S(1)}, u32[]{:S(2)}) copy-start(s32[256,1]{0,1:T(1,128)S(1)} %get-tuple-element.558) | copy-start | bytes 3076
  57.7 723.6 %copy-start.53 = (s32[256,1]{0,1:T(1,128)}, s32[256,1]{0,1:T(1,128)S(1)}, u32[]{:S(2)}) copy-start(s32[256,1]{0,1:T(1,128)S(1)} %get-tuple-element.559) | copy-start | bytes 3076
  57.7 723.6 %copy-start.55 = (s32[256,1]{0,1:T(1,128)}, s32[256,1]{0,1:T(1,128)S(1)}, u32[]{:S(2)}) copy-start(s32[256,1]{0,1:T(1,128)S(1)} %get-tuple-element.560) | copy-start | bytes 3076
  143.6 142.0 %all-to-all-start.2 = ((bf16[2,48,32,1024]{3,1,0,2:T(8,128)(2,1)}), bf16[2,48,32,1024]{3,1,0,2:T(8,128)(2,1)}, u32[]{:S(2)}, u32[]{:S(2)}) async-start(bf16[2,48,32,1024]{3,1,0,2:T(8,128)(2,1)} %copy.161), calls=%async_computation.2 | async-start | bytes 12582912 | tf_op jit(solution)/shard_map/all_to_all | solution.py:251
  148.4 286.0 %all-gather.7.cloned.1.call-start = ((), (), s32[]{:S(2)}) async-start(), calls=%async_computation.12 | async-start | bytes 5242880 | tf_op jit(solution)/shard_map/all_gather | solution.py:229
  285.6 142.0 %all-to-all-start = ((bf16[2,48,32,1024]{3,1,0,2:T(8,128)(2,1)}), bf16[2,48,32,1024]{3,1,0,2:T(8,128)(2,1)}, u32[]{:S(2)}, u32[]{:S(2)}) async-start(bf16[2,48,32,1024]{3,1,0,2:T(8,128)(2,1)} %copy.157), calls=%async_computation | async-start | bytes 12582912 | tf_op jit(solution)/shard_map/all_to_all | solution.py:227
  290.3 154.1 %all-gather.9.cloned.1.call-start = ((), (), s32[]{:S(2)}) async-start(), calls=%async_computation.13 | async-start | bytes 5242880 | tf_op jit(solution)/shard_map/all_gather | solution.py:230
  290.9 163.6 %all-gather.11.cloned.1.call-start = ((), (), s32[]{:S(2)}) async-start(), calls=%async_computation.14 | async-start | bytes 5242880 | tf_op jit(solution)/shard_map/all_gather | solution.py:231
  476.7 142.2 %all-to-all-start.1 = ((bf16[16,48,4,1024]{3,1,2,0:T(8,128)(2,1)}), bf16[16,48,4,1024]{3,1,2,0:T(8,128)(2,1)}, u32[]{:S(2)}, u32[]{:S(2)}) async-start(bf16[16,48,4,1024]{3,1,2,0:T(8,128)(2,1)} %copy.159), calls=%async_computation.1 | async-start | bytes 12582912 | tf_op jit(solution)/shard_map/all_to_all | solution.py:241
  514.0 109.6 %copy-start.19 = (s32[2,128,8]{2,1,0:T(8,128)S(1)}, s32[2,128,8]{2,1,0:T(8,128)}, u32[]{:S(2)}) copy-start(s32[2,128,8]{2,1,0:T(8,128)} %copy-done.18) | copy-start | bytes 24580
  514.0 109.7 %copy-start.40 = (s32[256]{0:T(256)S(1)}, s32[256]{0:T(256)}, u32[]{:S(2)}) copy-start(s32[256]{0:T(256)} %copy-done.39) | copy-start | bytes 3076
  514.0 110.0 %copy-start.31 = (s32[2,1024]{1,0:T(2,128)S(1)}, s32[2,1024]{1,0:T(2,128)}, u32[]{:S(2)}) copy-start(s32[2,1024]{1,0:T(2,128)} %copy-done.30) | copy-start | bytes 24580
  514.0 110.0 %copy-start.36 = (pred[256,8]{0,1:T(8,128)(4,1)S(1)}, pred[256,8]{0,1:T(8,128)(4,1)}, u32[]{:S(2)}) copy-start(pred[256,8]{0,1:T(8,128)(4,1)} %get-tuple-element.530) | copy-start | bytes 6148
  618.8 142.1 %all-to-all-start.3 = ((bf16[16,48,4,1024]{3,1,2,0:T(8,128)(2,1)}), bf16[16,48,4,1024]{3,1,2,0:T(8,128)(2,1)}, u32[]{:S(2)}, u32[]{:S(2)}) async-start(bf16[16,48,4,1024]{3,1,2,0:T(8,128)(2,1)} %copy.163), calls=%async_computation.3 | async-start | bytes 12582912 | tf_op jit(solution)/shard_map/all_to_all | solution.py:278
  623.6 321.3 %reduce-scatter.12.cloned.1.call-start = ((), (), s32[]{:S(2)}) async-start(), calls=%async_computation.15 | async-start | bytes 4718592 | tf_op jit(solution)/shard_map/reduce_scatter | solution.py:329
  664.5 123.7 %copy-start.26 = (bf16[256,32]{0,1:T(8,128)(2,1)}, bf16[256,32]{0,1:T(8,128)(2,1)S(1)}, u32[]{:S(2)}) copy-start(bf16[256,32]{0,1:T(8,128)(2,1)S(1)} %select_reduce_fusion.1) | copy-start | bytes 49156
  844.0 134.3 %reduce-scatter.22.cloned.1.call-start = ((), (), s32[]{:S(2)}) async-start(), calls=%async_computation.20 | async-start | bytes 5242880
  868.1 157.2 %reduce-scatter.24.cloned.1.call-start = ((), (), s32[]{:S(2)}) async-start(), calls=%async_computation.21 | async-start | bytes 5242880
  894.2 177.9 %reduce-scatter.20.cloned.1.call-start = ((), (), s32[]{:S(2)}) async-start(), calls=%async_computation.19 | async-start | bytes 5242880 | tf_op jit(solution)/shard_map/reduce_scatter | solution.py:286
  903.7 307.0 %reduce-scatter.18.cloned.1.call-start = ((), (), s32[]{:S(2)}) async-start(), calls=%async_computation.18 | async-start | bytes 540672 | tf_op jit(solution)/shard_map/reduce_scatter | solution.py:366
  905.9 446.7 %reduce-scatter.16.cloned.1.call-start = ((), (), s32[]{:S(2)}) async-start(), calls=%async_computation.17 | async-start | bytes 4325376 | tf_op jit(solution)/shard_map/reduce_scatter | solution.py:363
  908.7 592.7 %reduce-scatter.14.cloned.1.call-start = ((), (), s32[]{:S(2)}) async-start(), calls=%async_computation.16 | async-start | bytes 8650752 | tf_op jit(solution)/shard_map/reduce_scatter | solution.py:362
  1029.8 45.2 %copy-start.48 = (s32[256,1]{0,1:T(1,128)S(1)}, s32[256,1]{0,1:T(1,128)}, u32[]{:S(2)}) copy-start(s32[256,1]{0,1:T(1,128)} %copy-done.47) | copy-start | bytes 3076
  1029.8 45.2 %copy-start.50 = (s32[256,1]{0,1:T(1,128)S(1)}, s32[256,1]{0,1:T(1,128)}, u32[]{:S(2)}) copy-start(s32[256,1]{0,1:T(1,128)} %copy-done.49) | copy-start | bytes 3076
  1075.1 426.3 %copy-start.1 = (bf16[1024,1024]{1,0:T(8,128)(2,1)S(1)}, bf16[1024,1024]{1,0:T(8,128)(2,1)}, u32[]{:S(2)}) copy-start(bf16[1024,1024]{1,0:T(8,128)(2,1)} %param.22) | copy-start | bytes 6291460
  (63 other events, 1098.9 us)
Sparse Core Ops, SparseCore 0:
  17.4 75.4 all-gather.4
  844.1 87.3 reduce-scatter.11
  934.0 44.2 reduce-scatter.21
  980.7 44.5 reduce-scatter.23
  1027.7 44.4 reduce-scatter.19
  1074.8 135.8 reduce-scatter.17
  1213.6 138.9 reduce-scatter.15
  1355.5 145.9 reduce-scatter.13
Sparse Core Ops, SparseCore 1:
  150.4 36.1 all-gather.6
  292.4 36.1 all-gather.8
  330.0 34.3 all-gather.10
where the time goes:
time: 1520 us; the launch traced here: 1510 us
  waiting for transfers between devices  975 us (64%)
  matrix products  213 us (14%)
  local copies, waits for them, and re-layouts  182 us (12%)
  other arithmetic  61.3 us (4%)
  blocking collectives  39.4 us (3%)
  starting transfers between devices  20.5 us (1%)
  between operations  17.3 us (1%)
    reduce_scatter x1, waiting for transfers between devices, shards(): lax.psum_scatter(in_local, ('ctx', 'wsh'), scatter_dimension=0, tiled=True)  149 us
    reduce_scatter x1, waiting for transfers between devices, shards(): lax.psum_scatter(out_local, ('ctx', 'wsh'), scatter_dimension=0, tiled=True)  142 us
    all_to_all x1, waiting for transfers between devices, shards(): lax.all_to_all(sending, 'ctx', split_axis=2, concat_axis=0, tiled=True)  129 us
    all_to_all x1, waiting for transfers between devices, shards(): lax.all_to_all(grad_returned.reshape(SEQ_GRP, MOST, EXPERTS, D), 'ctx', s...  127 us
    all_to_all x1, waiting for transfers between devices, shards(): lax.all_to_all(produced, 'ctx', split_axis=0, concat_axis=2, tiled=True)  105 us
    all_to_all x1, waiting for transfers between devices, shards(): lax.all_to_all(grad_arrived, 'ctx', split_axis=0, concat_axis=2, tiled=True)  96.4 us
    reduce_scatter x1, waiting for transfers between devices, shards(): lax.psum_scatter(router_local, ('ctx', 'wsh'), scatter_dimension=0, tiled...  84.5 us
    unnamed x13, waiting for transfers between devices  67 us
  transfers between devices with their start and end apart: 15, of which 11 were waited for; matrix products, arithmetic and copies ran while one was open for 19% of the time, Pallas kernels for 0%

commit v1 on v0

--- a/solution.py
+++ b/solution.py
@@ -153,6 +153,11 @@
     return jnp.concatenate(
         [grad_keys.reshape(size, SEQ_GRP, -1), grad_values.reshape(size, SEQ_GRP, -1)], -1
     )
+
+
+def spread(local):
+    once = lax.psum_scatter(local, "ctx", scatter_dimension=0, tiled=True)
+    return lax.psum_scatter(once, "wsh", scatter_dimension=0, tiled=True).astype(jnp.float32)
 
 
 def shards(
@@ -202,80 +207,123 @@
     resid = inputs + jnp.dot(attended, out_weight, preferred_element_type=jnp.float32)
     scale_two = lax.rsqrt(jnp.mean(resid * resid, -1, keepdims=True) + EPS)
     normed_two = (resid * scale_two * second_gain).astype(jnp.bfloat16)
-    logits = jnp.dot(normed_two, router_weight, preferred_element_type=jnp.float32)
-    route_rows = routes.reshape(rows, TOP)
-    chosen = route_rows[..., None] == jnp.arange(EXPERTS, dtype=jnp.int32)
-    picked = jnp.sum(jnp.where(chosen, logits[:, None, :], 0.0), -1)
-    gates = jax.nn.softmax(picked, -1)
-    gates_low = gates.astype(jnp.bfloat16)
-    counts = chosen.reshape(SEQ_GRP, SEQ_TOK * TOP, EXPERTS).astype(jnp.int32)
-    ranks = jnp.sum((jnp.cumsum(counts, 1) - 1) * counts, -1).reshape(rows, TOP)
-    owner = (jnp.arange(rows, dtype=jnp.int32) // SEQ_TOK)[:, None]
-    slots = (owner * MOST + ranks) * EXPERTS + route_rows
-    slot_count = SEQ_GRP * MOST * EXPERTS
-    slot_ids = jnp.arange(slot_count, dtype=jnp.int32)[:, None]
-    dispatch = jnp.zeros((slot_count, rows), jnp.bfloat16)
-    combine = jnp.zeros((slot_count, rows), jnp.bfloat16)
-    for route_index in range(TOP):
-        match = slot_ids == slots[None, :, route_index]
-        dispatch = dispatch + match.astype(jnp.bfloat16)
-        combine = combine + jnp.where(
-            match, gates_low[None, :, route_index], jnp.zeros((), jnp.bfloat16)
-        )
-    sending = jnp.dot(dispatch, normed_two, preferred_element_type=jnp.float32).astype(jnp.bfloat16)
-    sending = sending.reshape(SEQ_GRP, MOST, EXPERTS, D)
-    arrived = lax.all_to_all(sending, "ctx", split_axis=2, concat_axis=0, tiled=True)
+    blocks = SEQ_GRP * ctx_count
+    mine = gate_weight.shape[0]
+    upstream = cotangent.reshape(rows, D)
+    cot_all = lax.all_gather(upstream, "ctx", axis=0, tiled=True)
+    chosen = jnp.any(
+        routes.reshape(rows, TOP).T[:, None, :] == jnp.arange(EXPERTS, dtype=jnp.int32)[:, None], 0
+    )
+    chosen_all = jnp.swapaxes(
+        lax.all_gather(chosen.astype(jnp.bfloat16), "ctx", axis=0, tiled=False), 0, 1
+    ).reshape(EXPERTS, blocks, SEQ_TOK)
     gate_full, up_full, down_full = (
         lax.all_gather(gate_weight, "wsh", axis=2, tiled=True),
         lax.all_gather(up_weight, "wsh", axis=2, tiled=True),
         lax.all_gather(down_weight, "wsh", axis=1, tiled=True),
     )
-    gate_act = jnp.einsum("rmxd,xdf->rmxf", arrived, gate_full, preferred_element_type=jnp.float32)
-    up_act = jnp.einsum("rmxd,xdf->rmxf", arrived, up_full, preferred_element_type=jnp.float32)
+    chosen_my = lax.dynamic_slice_in_dim(chosen_all, my_index * mine, mine, 0)
+    before = (
+        jnp.arange(SEQ_TOK, dtype=jnp.int32)[:, None] < jnp.arange(SEQ_TOK, dtype=jnp.int32)[None, :]
+    ).astype(jnp.bfloat16)
+    ranks = jnp.dot(
+        chosen_my.reshape(mine * blocks, SEQ_TOK), before, preferred_element_type=jnp.float32
+    ).reshape(mine, blocks, SEQ_TOK)
+    ranks = jnp.where(chosen_my > 0, ranks, -1.0)
+    normed_all = lax.all_gather(normed_two, "ctx", axis=0, tiled=True)
+    logits = lax.dot_general(
+        router_weight, normed_all, (((0,), (1,)), ((), ())), preferred_element_type=jnp.float32
+    )
+    taken = chosen_all.reshape(EXPERTS, blocks * SEQ_TOK) > 0
+    picked = jnp.where(taken, logits, NEG)
+    weights = jnp.where(taken, jnp.exp(picked - jnp.max(picked, 0, keepdims=True)), 0.0)
+    gates_all = weights / jnp.sum(weights, 0, keepdims=True)
+    gates = lax.dynamic_slice_in_dim(gates_all, my_index * rows, rows, 1)
+    gates_my = lax.dynamic_slice_in_dim(gates_all, my_index * mine, mine, 0).reshape(
+        mine, blocks, SEQ_TOK
+    )
+    slot_ids = jnp.arange(MOST, dtype=jnp.int32).astype(jnp.float32)
+    match = ranks[:, :, None, :] == slot_ids[:, None]
+    dispatch = match.astype(jnp.bfloat16)
+    combine = jnp.where(match, gates_my[:, :, None, :], 0.0).astype(jnp.bfloat16)
+    slot_gates = jnp.sum(jnp.where(match, gates_my[:, :, None, :], 0.0), -1).astype(jnp.bfloat16)
+    normed_blocks = normed_all.reshape(blocks, SEQ_TOK, D)
+    cot_blocks = cot_all.reshape(blocks, SEQ_TOK, D)
+    arrived = jnp.einsum(
+        "ebmt,btd->ebmd", dispatch, normed_blocks, preferred_element_type=jnp.float32
+    ).astype(jnp.bfloat16)
+    cot_slots = jnp.einsum(
+        "ebmt,btd->ebmd", dispatch, cot_blocks, preferred_element_type=jnp.float32
+    ).astype(jnp.bfloat16)
+    slots = blocks * MOST
+    arrived = arrived.reshape(mine, slots, D)
+    cot_slots = cot_slots.reshape(mine, slots, D)
+    grad_produced = cot_slots * slot_gates.reshape(mine, slots, 1)
+    gate_act = jnp.einsum("erd,edf->erf", arrived, gate_full, preferred_element_type=jnp.float32)
+    up_act = jnp.einsum("erd,edf->erf", arrived, up_full, preferred_element_type=jnp.float32)
     sigma = jax.nn.sigmoid(gate_act)
     swish = gate_act * sigma
     hidden = (swish * up_act).astype(jnp.bfloat16)
     produced = jnp.einsum(
-        "rmxf,xfd->rmxd", hidden, down_full, preferred_element_type=jnp.float32
-    ).astype(jnp.bfloat16)
-    returned = lax.all_to_all(produced, "ctx", split_axis=0, concat_axis=2, tiled=True)
-    returned_flat = returned.reshape(slot_count, D)
-    mixture = lax.dot_general(
-        combine, returned_flat, (((0,), (0,)), ((), ())), preferred_element_type=jnp.float32
-    )
-    layer_out = (resid + mixture).astype(jnp.bfloat16).reshape(SEQ_GRP, SEQ_TOK, D)
-    upstream = cotangent.reshape(rows, D)
-    grad_returned = jnp.dot(combine, upstream, preferred_element_type=jnp.float32).astype(
-        jnp.bfloat16
-    )
-    grad_produced = lax.all_to_all(
-        grad_returned.reshape(SEQ_GRP, MOST, EXPERTS, D),
+        "erf,efd->erd", hidden, down_full, preferred_element_type=jnp.float32
+    ).astype(jnp.bfloat16)
+    mixture = lax.psum_scatter(
+        jnp.einsum(
+            "ebmt,ebmd->btd",
+            combine,
+            produced.reshape(mine, blocks, MOST, D),
+            preferred_element_type=jnp.float32,
+        )
+        .astype(jnp.bfloat16)
+        .reshape(blocks * SEQ_TOK, D),
         "ctx",
-        split_axis=2,
-        concat_axis=0,
+        scatter_dimension=0,
         tiled=True,
     )
+    layer_out = (
+        (resid + mixture.astype(jnp.float32)).astype(jnp.bfloat16).reshape(SEQ_GRP, SEQ_TOK, D)
+    )
+    slot_dots = jnp.sum(
+        produced.astype(jnp.float32) * cot_slots.astype(jnp.float32), -1
+    ).reshape(mine, blocks, MOST)
+    gate_dots = jnp.sum(jnp.where(match, slot_dots[..., None], 0.0), 2)
+    gate_dots = jnp.swapaxes(gate_dots.reshape(mine, ctx_count, rows), 0, 1)
+    grad_gates = lax.all_to_all(gate_dots, "ctx", split_axis=0, concat_axis=0, tiled=True).reshape(
+        EXPERTS, rows
+    )
     down_local = jnp.einsum(
-        "rmxf,rmxd->xfd", hidden, grad_produced, preferred_element_type=jnp.float32
+        "erf,erd->efd", hidden, grad_produced, preferred_element_type=jnp.float32
     )
     grad_hidden = jnp.einsum(
-        "rmxd,xfd->rmxf", grad_produced, down_full, preferred_element_type=jnp.float32
+        "erd,efd->erf", grad_produced, down_full, preferred_element_type=jnp.float32
     ).astype(jnp.bfloat16)
     slope = sigma * (1.0 + gate_act * (1.0 - sigma))
     grad_gate = (grad_hidden * up_act * slope).astype(jnp.bfloat16)
     grad_up = (grad_hidden * swish).astype(jnp.bfloat16)
     gate_local = jnp.einsum(
-        "rmxd,rmxf->xdf", arrived, grad_gate, preferred_element_type=jnp.float32
-    )
-    up_local = jnp.einsum("rmxd,rmxf->xdf", arrived, grad_up, preferred_element_type=jnp.float32)
+        "erd,erf->edf", arrived, grad_gate, preferred_element_type=jnp.float32
+    )
+    up_local = jnp.einsum("erd,erf->edf", arrived, grad_up, preferred_element_type=jnp.float32)
     grad_arrived = jnp.einsum(
-        "rmxf,xdf->rmxd", grad_gate, gate_full, preferred_element_type=jnp.float32
+        "erf,edf->erd", grad_gate, gate_full, preferred_element_type=jnp.float32
     )
     grad_arrived = (
         grad_arrived
-        + jnp.einsum("rmxf,xdf->rmxd", grad_up, up_full, preferred_element_type=jnp.float32)
-    ).astype(jnp.bfloat16)
-    grad_sent = lax.all_to_all(grad_arrived, "ctx", split_axis=0, concat_axis=2, tiled=True)
+        + jnp.einsum("erf,edf->erd", grad_up, up_full, preferred_element_type=jnp.float32)
+    ).astype(jnp.bfloat16)
+    grad_sent = lax.psum_scatter(
+        jnp.einsum(
+            "ebmt,ebmd->btd",
+            dispatch,
+            grad_arrived.reshape(mine, blocks, MOST, D),
+            preferred_element_type=jnp.float32,
+        )
+        .astype(jnp.bfloat16)
+        .reshape(blocks * SEQ_TOK, D),
+        "ctx",
+        scatter_dimension=0,
+        tiled=True,
+    )
     gate_grad, up_grad, down_grad = (
         lax.psum_scatter(
             gate_local.astype(jnp.bfloat16), "wsh", scatter_dimension=2, tiled=True
@@ -287,21 +335,14 @@
             down_local.astype(jnp.bfloat16), "wsh", scatter_dimension=1, tiled=True
         ).astype(jnp.float32),
     )
-    grad_normed_two = lax.dot_general(
-        dispatch,
-        grad_sent.reshape(slot_count, D),
-        (((0,), (0,)), ((), ())),
-        preferred_element_type=jnp.float32,
-    )
-    picked_rows = jnp.take(returned_flat, slots.reshape(-1), axis=0).reshape(rows, TOP, D)
-    grad_gates = jnp.einsum("tkd,td->tk", picked_rows, upstream, preferred_element_type=jnp.float32)
-    grad_picked = gates * (grad_gates - jnp.sum(gates * grad_gates, -1, keepdims=True))
-    grad_logits = jnp.sum(jnp.where(chosen, grad_picked[..., None], 0.0), 1).astype(jnp.bfloat16)
+    grad_logits = (gates * (grad_gates - jnp.sum(gates * grad_gates, 0, keepdims=True))).astype(
+        jnp.bfloat16
+    )
     router_local = lax.dot_general(
-        normed_two, grad_logits, (((0,), (0,)), ((), ())), preferred_element_type=jnp.float32
-    )
-    grad_normed_two = grad_normed_two + lax.dot_general(
-        grad_logits, router_weight, (((1,), (1,)), ((), ())), preferred_element_type=jnp.float32
+        normed_two, grad_logits, (((0,), (1,)), ((), ())), preferred_element_type=jnp.float32
+    )
+    grad_normed_two = grad_sent.astype(jnp.float32) + lax.dot_general(
+        grad_logits, router_weight, (((0,), (1,)), ((), ())), preferred_element_type=jnp.float32
     )
     grad_resid_norm, second_local = norm_back(resid, scale_two, second_gain, grad_normed_two)
     grad_resid = upstream.astype(jnp.float32) + grad_resid_norm
@@ -358,13 +399,12 @@
     )
     grad_inputs_norm, first_local = norm_back(inputs, scale_one, first_gain, grad_normed)
     tokens_grad = (grad_resid + grad_inputs_norm).astype(jnp.bfloat16).reshape(SEQ_GRP, SEQ_TOK, D)
-    in_grad, out_grad, first_gain_grad, second_gain_grad, router_grad = (
-        lax.psum_scatter(in_local, ("ctx", "wsh"), scatter_dimension=0, tiled=True),
-        lax.psum_scatter(out_local, ("ctx", "wsh"), scatter_dimension=0, tiled=True),
-        lax.psum_scatter(first_local, ("ctx", "wsh"), scatter_dimension=0, tiled=True),
-        lax.psum_scatter(second_local, ("ctx", "wsh"), scatter_dimension=0, tiled=True),
-        lax.psum_scatter(router_local, ("ctx", "wsh"), scatter_dimension=0, tiled=True),
-    )
+    in_grad, out_grad = spread(in_local.astype(jnp.bfloat16)), spread(out_local.astype(jnp.bfloat16))
+    small = spread(
+        jnp.concatenate([router_local, first_local[:, None], second_local[:, None]], -1)
+    )
+    router_grad = small[:, :EXPERTS]
+    first_gain_grad, second_gain_grad = small[:, EXPERTS], small[:, EXPERTS + 1]
     return (
         layer_out,
         tokens_grad,

time: 1520 us -> 1200 us (0.79)
  waiting for transfers between devices: 975 us -> 762 us
  local copies, waits for them, and re-layouts: 182 us -> 98 us
    all_to_all x4 -> x1, waiting for transfers between devices: 457 us -> 7.2 us  [shards(): lax.all_to_all(gate_dots, 'ctx', split_axis=0, concat_axis=0, tiled=True)]
    all_gather x0 -> x2, waiting for transfers between devices: none -> 56.8 us  [the longest x1 56.8 us: shards(): normed_all = lax.all_gather(normed_two, 'ctx', axis=0, tiled=True)]
    reduce_scatter x1, waiting for transfers between devices: 0.02 us -> 50.6 us  [shards(): lax.psum_scatter(terms.reshape(SEQ_TOK * lax.axis_size('ctx'), SEQ_GRP, t...]
    unnamed x13 -> x21, waiting for transfers between devices: 67 us -> 110 us
    unnamed x1 -> x0, blocking collectives: 39.4 us -> none
    all_gather x1, waiting for transfers between devices: 35.2 us -> 72 us  [shards(): whole = lax.all_gather(key_value, 'ctx', axis=0, tiled=True)]
    all_to_all x4 -> x0, local copies, waits for them, and re-layouts: 34 us -> none  [the longest x1 10.3 us: shards(): lax.all_to_all(grad_arrived, 'ctx', split_axis=0, concat_axis=2, tiled=True)]
    reshape x7 -> x3, local copies, waits for them, and re-layouts: 32.7 us -> 0.07 us  [the longest x1 0.05 us: shards(): chosen_all = jnp.swapaxes(lax.all_gather(chosen.astype(jnp.bfloat16), 'ct...]
  transfers between devices with their start and end apart: 15 -> 19, of which waited for: 11 -> 18; matrix products, arithmetic and copies ran while one was open for 19% -> 19% of each run, Pallas kernels for 0% -> 0%
where the time goes in v1:
time: 1200 us; the launch traced here: 1190 us
  waiting for transfers between devices  762 us (64%)
  matrix products  226 us (19%)
  local copies, waits for them, and re-layouts  98 us (8%)
  other arithmetic  47.1 us (4%)
  blocking collectives  31.4 us (3%)
  between operations  15.2 us (1%)
    reduce_scatter x3, waiting for transfers between devices, spread(): once = lax.psum_scatter(local, 'ctx', scatter_dimension=0, tiled=True)  149 us
    unnamed x21, waiting for transfers between devices  110 us
    reduce_scatter x1, waiting for transfers between devices, shards(): lax.psum_scatter(jnp.einsum('ebmt,ebmd->btd', combine, produced.reshape(m...  88.2 us
    all_gather x1, waiting for transfers between devices, shards(): whole = lax.all_gather(key_value, 'ctx', axis=0, tiled=True)  72 us
    reduce_scatter x1, waiting for transfers between devices, shards(): lax.psum_scatter(jnp.einsum('ebmt,ebmd->btd', dispatch, grad_arrived.resh...  69.5 us
    all_gather x1, waiting for transfers between devices, shards(): normed_all = lax.all_gather(normed_two, 'ctx', axis=0, tiled=True)  56.8 us
    reduce_scatter x1, waiting for transfers between devices, shards(): lax.psum_scatter(terms.reshape(SEQ_TOK * lax.axis_size('ctx'), SEQ_GRP, t...  50.6 us
    unnamed x71, local copies, waits for them, and re-layouts  48.8 us
  transfers between devices with their start and end apart: 19, of which 18 were waited for; matrix products, arithmetic and copies ran while one was open for 19% of the time, Pallas kernels for 0%

profile of v1, /device:TPU:0, one launch (start us, length us, event | category | flops | bytes accessed | tf_op | source)
XLA Modules:
  0.0 1186.8 jit_solution(15257794818544734829)
XLA Ops:
  25.5 72.0 %all-gather.8.cloned.1.call-done = bf16[1024,2,1024]{2,0,1:T(8,128)(2,1)} async-done(((bf16[128,2,1024]{2,0,1:T(8,128)(2,1)}), bf16[1024,2,1024]{2,0,1:T(8,128)(2,1)}) %all-gather.8.cloned.1.call-update) | async-done | bytes 4194320 | tf_op jit(solution)/shard_map/all_gather | solution.py:204
  103.8 22.8 %while.47 = (s32[]{:T(128)}, f32[2,8,2,128]{3,2,1,0:T(2,128)S(1)}, f32[2,8,2,128]{3,2,1,0:T(2,128)S(1)}, s32[2,512]{1,0:T(2,128)S(1)}, bf16[2,512,2,1024]{1,3,2,...) while((s32[]{:T(128)}, f32[2,8,2,128]{3,2,1,0:T(2,128)S(1)}, ...), condition=%wide.region_4.5_spmd.clone, body=%wide.region_1.4_spmd.clone.sunk | while | flops 285302400 | bytes 25058420 | solution.py:88
  126.6 17.0 %while.48 = (s32[]{:T(128)}, f32[2,128,8,2,64]{1,4,3,2,0:T(8,128)}, bf16[2,512,2,1024]{1,3,2,0:T(8,128)(2,1)}, s32[2,512]{1,0:T(2,128)S(1)}, bf16[2,128,8,2,64]{...) while((s32[]{:T(128)}, f32[2,128,8,2,64]{1,4,3,2,0:T(8,128)}, ...), condition=%wide.region_6.7_spmd.clone, body=%wide.region_5.6_spmd.clone.sunk | while | flops 545853056 | bytes 13261939 | solution.py:102
  150.2 31.4 %all-gather = bf16[256,256]{1,0:T(8,128)(2,1)S(1)} all-gather(bf16[32,256]{1,0:T(8,128)(2,1)S(1)} %convert_element_type.242), channel_id=2, replica_groups=mesh['ctx'=8,'wsh'=4] {'ctx'}, dimensions={0}, use_global_device_ids=true | all-gather | bytes 147456 | tf_op jit(solution)/shard_map/all_gather | solution.py:218
  189.5 56.8 %all-gather.10.cloned.1.call-done = bf16[2048,1024]{1,0:T(8,128)(2,1)} async-done(((bf16[256,1024]{1,0:T(8,128)(2,1)}), bf16[2048,1024]{1,0:T(8,128)(2,1)}) %all-gather.10.cloned.1.call-update) | async-done | bytes 4194320 | tf_op jit(solution)/shard_map/all_gather | solution.py:233
  253.7 27.5 %all-gather.12.cloned.1.call-done = bf16[4,1024,512]{2,1,0:T(8,128)(2,1)} async-done(((bf16[4,1024,128]{2,1,0:T(8,128)(2,1)}), bf16[4,1024,512]{2,1,0:T(8,128)(2,1)}) %all-gather.12.cloned.1.call-update) | async-done | bytes 4194320 | tf_op jit(solution)/shard_map/all_gather | solution.py:221
  281.2 10.4 fusion.143
  291.6 26.1 %all-gather.14.cloned.1.call-done = bf16[4,1024,512]{2,1,0:T(8,128)(2,1)} async-done(((bf16[4,1024,128]{2,1,0:T(8,128)(2,1)}), bf16[4,1024,512]{2,1,0:T(8,128)(2,1)}) %all-gather.14.cloned.1.call-update) | async-done | bytes 4194320 | tf_op jit(solution)/shard_map/all_gather | solution.py:222
  317.7 13.4 %multiply_convert_fusion = (bf16[4,768,512]{2,1,0:T(8,128)(2,1)}, f32[4,768,512]{2,1,0:T(8,128)}) fusion(f32[4,768,512]{2,1,0:T(8,128)} %fusion.143, bf16[4,768,1024]{2,1,0:T(8,128)(2,1)} %bitcast.429, bf16[4,1024,512]{2,1,0:T(8,128)(2,1)} %all-gather.14.cloned.1.call-done), kind=kOutput, calls=%fused_computation.108 | convolution fusion | flops 3230662656 | bytes 26214400 | tf_op jit(solution)/shard_map/erd,edf->erf/dot_general | solution.py:263
  331.1 22.5 %all-gather.16.cloned.1.call-done = bf16[4,512,1024]{2,1,0:T(8,128)(2,1)} async-done(((bf16[4,128,1024]{2,1,0:T(8,128)(2,1)}), bf16[4,512,1024]{2,1,0:T(8,128)(2,1)}) %all-gather.16.cloned.1.call-update) | async-done | bytes 4194320 | tf_op jit(solution)/shard_map/all_gather | solution.py:223
  353.6 11.6 multiply_reduce_fusion
  376.1 14.9 %fusion.67 = (bf16[4,768,512]{2,1,0:T(8,128)(2,1)}, bf16[4,768,512]{2,1,0:T(8,128)(2,1)}) fusion(f32[4,768,512]{2,1,0:T(8,128)} %get-tuple-element.607, f32[4,768,512]{2,1,0:T(8,128)} %fusion.143, bf16[4,768,1024]{2,1,0:T(8,128)(2,1)} %bitcast_multiply_fusion.1, bf16[4,512,1024]{2,1,0:T(8,128)(2,1)} %all-gather.16.cloned.1.call-done), kind=kOutput, calls=%fused_computation.100 | convolution fusion | flops 3240099840 | bytes 29360128 | tf_op jit(solution)/shard_map/erd,efd->erf/dot_general | solution.py:297
  391.0 11.3 fusion.144
  402.3 11.7 add_convert_fusion
  439.9 69.5 %reduce-scatter.21.cloned.1.call-done = bf16[256,1024]{1,0:T(8,128)(2,1)} async-done(((bf16[2048,1024]{1,0:T(8,128)(2,1)}), bf16[256,1024]{1,0:T(8,128)(2,1)}) %reduce-scatter.21.cloned.1.call-update) | async-done | bytes 524304 | tf_op jit(solution)/shard_map/reduce_scatter | solution.py:314
  512.8 88.2 %reduce-scatter.19.cloned.1.call-done = bf16[256,1024]{1,0:T(8,128)(2,1)} async-done(((bf16[2048,1024]{1,0:T(8,128)(2,1)}), bf16[256,1024]{1,0:T(8,128)(2,1)}) %reduce-scatter.19.cloned.1.call-update) | async-done | bytes 524304 | tf_op jit(solution)/shard_map/reduce_scatter | solution.py:270
  607.0 52.6 %while.46 = (s32[]{:T(128)}, bf16[2,512,2,1024]{3,1,0,2:T(8,128)(2,1)}, s32[2,512]{1,0:T(2,128)S(1)}, bf16[2,512,2,1024]{1,3,2,0:T(8,128)(2,1)}, bf16[2,128,8,2,...) while((s32[]{:T(128)}, ...), condition=%wide.region_21.22_spmd.clone, body=%wide.region_20.21_spmd.clone.sunk | while | flops 1100025472 | bytes 61071016 | solution.py:365
  663.2 31.6 %while.49 = (s32[]{:T(128)}, f32[2,128,8,2,64]{1,4,3,2,0:T(8,128)}, bf16[2,512,2,1024]{1,3,2,0:T(8,128)(2,1)}, s32[2,512]{1,0:T(2,128)S(1)}, bf16[2,128,8,2,64]{...) while((s32[]{:T(128)}, f32[2,128,8,2,64]{1,4,3,2,0:T(8,128)}, ...), condition=%wide.region_19.20_spmd.clone, body=%wide.region_18.19_spmd.clone.sunk | while | flops 818482816 | bytes 40017080 | solution.py:132
  686.6 8.2 fusion.251
  697.1 50.6 %reduce-scatter.23.cloned.1.call-done = bf16[128,2,1024]{2,0,1:T(8,128)(2,1)} async-done(((bf16[1024,2,1024]{2,0,1:T(8,128)(2,1)}), bf16[128,2,1024]{2,0,1:T(8,128)(2,1)}) %reduce-scatter.23.cloned.1.call-update) | async-done | bytes 524304 | tf_op jit(solution)/shard_map/reduce_scatter | solution.py:370
  758.8 11.2 convolution_convert_fusion.3
  770.0 8.1 copy.211
  784.9 9.2 convolution_convert_fusion.4
  808.6 9.2 convolution_convert_fusion.2
  819.9 57.8 %reduce-scatter.33.cloned.1.call-done = f32[128,34]{0,1:T(8,128)} async-done(((f32[1024,34]{0,1:T(8,128)}), f32[128,34]{0,1:T(8,128)}) %reduce-scatter.33.cloned.1.call-update) | async-done | bytes 17424 | tf_op jit(solution)/shard_map/reduce_scatter | solution.py:159
  879.4 89.1 %reduce-scatter.25.cloned.1.call-done = bf16[128,2048]{1,0:T(8,128)(2,1)} async-done(((bf16[1024,2048]{1,0:T(8,128)(2,1)}), bf16[128,2048]{1,0:T(8,128)(2,1)}) %reduce-scatter.25.cloned.1.call-update) | async-done | bytes 524304 | tf_op jit(solution)/shard_map/reduce_scatter | solution.py:159
  968.6 46.7 %reduce-scatter.41.cloned.1.call-done = bf16[128,4096]{1,0:T(8,128)(2,1)} async-done(((bf16[512,4096]{1,0:T(8,128)(2,1)}), bf16[128,4096]{1,0:T(8,128)(2,1)}) %reduce-scatter.41.cloned.1.call-update) | async-done | bytes 1048592
  1019.6 42.7 %reduce-scatter.39.cloned.1.call-done = bf16[128,4096]{1,0:T(8,128)(2,1)} async-done(((bf16[512,4096]{1,0:T(8,128)(2,1)}), bf16[128,4096]{1,0:T(8,128)(2,1)}) %reduce-scatter.39.cloned.1.call-update) | async-done | bytes 1048592
  1068.7 40.5 %reduce-scatter.35.cloned.1.call-done = bf16[4,128,1024]{2,1,0:T(8,128)(2,1)} async-done(((bf16[4,512,1024]{2,1,0:T(8,128)(2,1)}), bf16[4,128,1024]{2,1,0:T(8,128)(2,1)}) %reduce-scatter.35.cloned.1.call-update) | async-done | bytes 1048592 | tf_op jit(solution)/shard_map/reduce_scatter | solution.py:334
  1112.0 19.6 %reduce-scatter.31.cloned.1.call-done = bf16[32,1024]{1,0:T(8,128)(2,1)} async-done(((bf16[128,1024]{1,0:T(8,128)(2,1)}), bf16[32,1024]{1,0:T(8,128)(2,1)}) %reduce-scatter.31.cloned.1.call-update) | async-done | bytes 65552 | tf_op jit(solution)/shard_map/reduce_scatter | solution.py:160
  1135.6 18.4 %reduce-scatter.37.cloned.1.call-done = f32[32,34]{1,0:T(8,128)} async-done(((f32[128,34]{1,0:T(8,128)}), f32[32,34]{1,0:T(8,128)}) %reduce-scatter.37.cloned.1.call-update) | async-done | bytes 4368
  1156.1 22.0 %reduce-scatter.27.cloned.1.call-done = bf16[32,2048]{1,0:T(8,128)(2,1)} async-done(((bf16[128,2048]{1,0:T(8,128)(2,1)}), bf16[32,2048]{1,0:T(8,128)(2,1)}) %reduce-scatter.27.cloned.1.call-update) | async-done | bytes 131088 | tf_op jit(solution)/shard_map/reduce_scatter | solution.py:160
  (286 shorter events, 270.2 us)
Async XLA Ops:
  7.2 138.4 %copy-start = (bf16[1024,1024]{1,0:T(8,128)(2,1)S(1)}, bf16[1024,1024]{1,0:T(8,128)(2,1)}, u32[]{:S(2)}) copy-start(bf16[1024,1024]{1,0:T(8,128)(2,1)} %param.22) | copy-start | bytes 6291460
  7.2 90.4 %all-gather.8.cloned.1.call-start = ((), (), s32[]{:S(2)}) async-start(), calls=%async_computation.13 | async-start | bytes 4718592 | tf_op jit(solution)/shard_map/all_gather | solution.py:204
  21.9 160.1 %all-gather.18.cloned.1.call-start = ((), (), s32[]{:S(2)}) async-start(), calls=%async_computation.19 | async-start | bytes 4718592 | tf_op jit(solution)/shard_map/all_gather | solution.py:213
  22.7 223.6 %all-gather.10.cloned.1.call-start = ((), (), s32[]{:S(2)}) async-start(), calls=%async_computation.14 | async-start | bytes 4718592 | tf_op jit(solution)/shard_map/all_gather | solution.py:233
  126.6 19.0 %copy-start.10 = (bf16[2,128,1024]{2,1,0:T(8,128)(2,1)S(1)}, bf16[2,128,1024]{2,1,0:T(8,128)(2,1)}, u32[]{:S(2)}) copy-start(bf16[2,128,1024]{2,1,0:T(8,128)(2,1)} %param.19) | copy-start | bytes 1572868
  148.4 132.8 %all-gather.12.cloned.1.call-start = ((), (), s32[]{:S(2)}) async-start(), calls=%async_computation.15 | async-start | bytes 5242880 | tf_op jit(solution)/shard_map/all_gather | solution.py:221
  149.0 168.7 %all-gather.14.cloned.1.call-start = ((), (), s32[]{:S(2)}) async-start(), calls=%async_computation.16 | async-start | bytes 5242880 | tf_op jit(solution)/shard_map/all_gather | solution.py:222
  149.6 204.0 %all-gather.16.cloned.1.call-start = ((), (), s32[]{:S(2)}) async-start(), calls=%async_computation.17 | async-start | bytes 5242880 | tf_op jit(solution)/shard_map/all_gather | solution.py:223
  150.1 359.3 %reduce-scatter.21.cloned.1.call-start = ((), (), s32[]{:S(2)}) async-start(), calls=%async_computation.20 | async-start | bytes 4718592 | tf_op jit(solution)/shard_map/reduce_scatter | solution.py:314
  353.6 11.7 copy-start.20
  391.0 11.3 copy-start.31
  420.2 180.8 %reduce-scatter.19.cloned.1.call-start = ((), (), s32[]{:S(2)}) async-start(), calls=%async_computation.18 | async-start | bytes 4718592 | tf_op jit(solution)/shard_map/reduce_scatter | solution.py:270
  426.4 174.6 %copy-start.17 = (bf16[2,128,1024]{2,1,0:T(8,128)(2,1)S(1)}, bf16[2,128,1024]{2,1,0:T(8,128)(2,1)}, u32[]{:S(2)}) copy-start(bf16[2,128,1024]{2,1,0:T(8,128)(2,1)} %param.29) | copy-start | bytes 1572868
  427.1 12.8 %all-to-all-start = ((f32[8,4,256]{2,1,0:T(4,128)}), f32[8,4,256]{2,1,0:T(4,128)S(1)}, u32[]{:S(2)}, u32[]{:S(2)}) async-start(f32[8,4,256]{2,1,0:T(4,128)} %copy.165), calls=%async_computation.2 | async-start | bytes 65536 | tf_op jit(solution)/shard_map/all_to_all | solution.py:291
  432.6 315.1 %reduce-scatter.23.cloned.1.call-start = ((), (), s32[]{:S(2)}) async-start(), calls=%async_computation.21 | async-start | bytes 4718592 | tf_op jit(solution)/shard_map/reduce_scatter | solution.py:370
  659.6 160.2 %reduce-scatter.29.cloned.1.call-start = ((), (), s32[]{:S(2)}) async-start(), calls=%async_computation.24 | async-start | bytes 2359296 | tf_op jit(solution)/shard_map/reduce_scatter | solution.py:159
  663.2 214.5 %reduce-scatter.33.cloned.1.call-start = ((), (), s32[]{:S(2)}) async-start(), calls=%async_computation.26 | async-start | bytes 184320 | tf_op jit(solution)/shard_map/reduce_scatter | solution.py:159
  663.2 33.0 %copy-start.19 = (f32[128,32]{0,1:T(8,128)S(1)}, f32[128,32]{0,1:T(8,128)}, u32[]{:S(2)}) copy-start(f32[128,32]{0,1:T(8,128)} %copy-done.18) | copy-start | bytes 49156
  663.2 33.0 %copy-start.21 = (f32[128,32]{0,1:T(8,128)S(1)}, f32[128,32]{0,1:T(8,128)}, u32[]{:S(2)}) copy-start(f32[128,32]{0,1:T(8,128)} %get-tuple-element.597) | copy-start | bytes 49156
  696.4 53.2 %copy-start.11 = (bf16[2,128,1024]{2,1,0:T(8,128)(2,1)S(1)}, bf16[2,128,1024]{2,1,0:T(8,128)(2,1)}, u32[]{:S(2)}) copy-start(bf16[2,128,1024]{2,1,0:T(8,128)(2,1)} %param.19) | copy-start | bytes 1572868
  696.4 53.2 %copy-start.29 = (f32[256]{0:T(256)S(1)}, f32[256]{0:T(256)}, u32[]{:S(2)}) copy-start(f32[256]{0:T(256)} %get-tuple-element.595) | copy-start | bytes 3076
  696.4 53.2 %copy-start.30 = (f32[1024]{0:T(1024)S(1)}, f32[1024]{0:T(1024)}, u32[]{:S(2)}) copy-start(f32[1024]{0:T(1024)} %param.23) | copy-start | bytes 12292
  754.9 213.6 %reduce-scatter.25.cloned.1.call-start = ((), (), s32[]{:S(2)}) async-start(), calls=%async_computation.22 | async-start | bytes 4718592 | tf_op jit(solution)/shard_map/reduce_scatter | solution.py:159
  758.3 257.1 %reduce-scatter.41.cloned.1.call-start = ((), (), s32[]{:S(2)}) async-start(), calls=%async_computation.30 | async-start | bytes 5242880
  784.6 277.7 %reduce-scatter.39.cloned.1.call-start = ((), (), s32[]{:S(2)}) async-start(), calls=%async_computation.29 | async-start | bytes 5242880
  808.6 300.6 %reduce-scatter.35.cloned.1.call-start = ((), (), s32[]{:S(2)}) async-start(), calls=%async_computation.27 | async-start | bytes 5242880 | tf_op jit(solution)/shard_map/reduce_scatter | solution.py:334
  817.9 150.7 %copy-start.27 = (f32[2,128]{1,0:T(2,128)S(1)}, f32[2,128]{1,0:T(2,128)}, u32[]{:S(2)}) copy-start(f32[2,128]{1,0:T(2,128)} %copy-done.26) | copy-start | bytes 3076
  817.9 313.7 %reduce-scatter.31.cloned.1.call-start = ((), (), s32[]{:S(2)}) async-start(), calls=%async_computation.25 | async-start | bytes 327680 | tf_op jit(solution)/shard_map/reduce_scatter | solution.py:160
  819.8 334.2 %reduce-scatter.37.cloned.1.call-start = ((), (), s32[]{:S(2)}) async-start(), calls=%async_computation.28 | async-start | bytes 81920
  879.2 298.9 %reduce-scatter.27.cloned.1.call-start = ((), (), s32[]{:S(2)}) async-start(), calls=%async_computation.23 | async-start | bytes 655360 | tf_op jit(solution)/shard_map/reduce_scatter | solution.py:160
  1064.2 69.0 %copy-start.8 = (f32[256,1024]{1,0:T(8,128)S(1)}, f32[256,1024]{1,0:T(8,128)}, u32[]{:S(2)}) copy-start(f32[256,1024]{1,0:T(8,128)} %copy-done.6) | copy-start | bytes 3145732
  1065.9 113.9 %copy-start.1 = (bf16[1024,1024]{1,0:T(8,128)(2,1)S(1)}, bf16[1024,1024]{1,0:T(8,128)(2,1)}, u32[]{:S(2)}) copy-start(bf16[1024,1024]{1,0:T(8,128)(2,1)} %param.22) | copy-start | bytes 6291460
  (24 other events, 82.4 us)
Sparse Core Ops, SparseCore 0:
  22.0 75.4 all-gather.7
  99.7 72.5 all-gather.17
  175.0 71.2 all-gather.9
  247.7 33.5 all-gather.11
  282.6 34.9 all-gather.13
  319.1 34.4 all-gather.15
  420.3 89.0 reduce-scatter.20
  513.0 87.9 reduce-scatter.18
  659.8 87.9 reduce-scatter.22
  751.7 68.0 reduce-scatter.28
  823.5 54.1 reduce-scatter.32
  881.2 87.3 reduce-scatter.24
  971.1 44.1 reduce-scatter.40
  1017.7 44.5 reduce-scatter.38
  1064.7 44.4 reduce-scatter.34
  1111.5 20.0 reduce-scatter.30
  1134.5 19.5 reduce-scatter.36
  1156.4 21.6 reduce-scatter.26
